TPU v7x, 256 devices: a whole 4x4x8 slice. The times are simulated.
256 devices in a mesh: row: 16 (over x, z_lo), col: 16 (over z_hi, y, core).
Axes of the slice: x: 4, y: 4, z: 8 (z_hi: 2, z_lo: 4; z = z_hi * 4 + z_lo), core: 2. Of those that a mesh axis runs over, the one named last changes fastest.
Arguments:
- factors: bfloat16 [32768, 256], P(('row', 'col')), may hold values from -1.5 to 1.5
- cores: bfloat16 [8, 256, 256], replicated, may hold values from -0.375 to 0.375
- tiles: bfloat16 [8192, 256, 256], P(('row', 'col')), may hold values from -6 to 6
- tile_coords: int32 [8192, 3], P(('row', 'col')), may hold values from 0 to 7, as said below
- tile_counts: int32 [256], P(('row', 'col')), may hold values from 1 to 32, as said below
Outputs:
- gradient: float32 [32768, 256], P(('row', 'col'))
Inputs may be any that keep to these rules, and one draw needn't show every extreme that they name: `tile_coords`: column 0 is a relation below 8, column 1 below 8, column 2 below 8; within one device no two slots have the same three coordinates. `tile_counts`: some device has all 32 slots live.
All inputs are finite; a program needn't handle non-finite values.
Results may differ from a plain program's by a relative error of at most 0.0011.
Values may be sent and summed in bfloat16 or wider, within the bound.
A program may use at most 128 MiB of HBM per device.

v0:
```python
import jax
import jax.numpy as jnp
from jax import lax
from jax.sharding import PartitionSpec as P

weight_decay = 1.0


def broadcast(value, axis, source):
    kept = jnp.where(lax.axis_index(axis) == source, value, 0).astype(value.dtype)
    return lax.psum(kept, axis)


def local(factors, cores, tiles, tile_coords, tile_counts):
    n_row = lax.axis_size("row")
    n_col = lax.axis_size("col")
    row_ratio = n_row // n_col
    shard_rows, rank_width = factors.shape
    tile_size = tiles.shape[1]
    relations = cores.shape[0]
    src_rows = shard_rows * n_col
    tgt_rows = src_rows * row_ratio
    src_blocks = src_rows // tile_size
    tgt_blocks = tgt_rows // tile_size
    row_pos = lax.axis_index("row")
    col_pos = lax.axis_index("col")
    source = lax.all_gather(factors, "col", axis=0, tiled=True)
    received = broadcast(source, "row", col_pos * row_ratio + 0)
    left_core = jnp.einsum("nr,krs->kns", source, cores, preferred_element_type=jnp.float32).astype(
        jnp.bfloat16
    )
    left_core = left_core.reshape(relations, src_blocks, tile_size, rank_width)
    right_core = jnp.einsum(
        "nr,ksr->kns", received, cores, preferred_element_type=jnp.float32
    ).astype(jnp.bfloat16)
    right_core = right_core.reshape(relations, tgt_blocks, tile_size, rank_width)
    tgt_factor = received.reshape(tgt_blocks, tile_size, rank_width)
    live_count = tile_counts[0]

    def group_pass(group, carry):
        grad_src, grad_tgt = carry
        start = group * 8
        coords = lax.dynamic_slice_in_dim(tile_coords, start, 8, 0)
        values = lax.dynamic_slice_in_dim(tiles, start, 8, 0)
        is_live = start + jnp.arange(8, dtype=jnp.int32) < live_count
        relation = coords[:, 0]
        src_index = coords[:, 1]
        tgt_index = coords[:, 2]
        left = left_core[relation, src_index]
        right = tgt_factor[tgt_index]
        right_rel = right_core[relation, tgt_index]
        predicted = jnp.einsum("gtr,gur->gtu", left, right, preferred_element_type=jnp.float32)
        resid = jnp.where(
            is_live[:, None, None], values.astype(jnp.float32) - predicted, 0.0
        ).astype(jnp.bfloat16)
        src_grad = jnp.einsum("gtu,gur->gtr", resid, right_rel, preferred_element_type=jnp.float32)
        tgt_grad = jnp.einsum("gtu,gtr->gur", resid, left, preferred_element_type=jnp.float32)
        return (grad_src.at[src_index].add(src_grad), grad_tgt.at[tgt_index].add(tgt_grad))

    start_grads = (
        jnp.zeros((src_blocks, tile_size, rank_width), jnp.float32),
        jnp.zeros((tgt_blocks, tile_size, rank_width), jnp.float32),
    )
    grad_src, grad_tgt = lax.fori_loop(0, (live_count + 7) // 8, group_pass, start_grads)
    grad_src = grad_src.reshape(src_rows, rank_width)
    grad_tgt = grad_tgt.reshape(tgt_rows, rank_width)
    tgt_total = lax.psum(grad_tgt, "row")
    summed = lax.psum_scatter(grad_src, "col", scatter_dimension=0, tiled=True)
    relay_block = broadcast(tgt_total, "col", row_pos // row_ratio)
    relay_part = lax.dynamic_slice_in_dim(
        relay_block, (row_pos % row_ratio * n_col + col_pos) * shard_rows, shard_rows, 0
    )
    summed = summed + relay_part
    return weight_decay * factors.astype(jnp.float32) - summed / tile_size


def solution(mesh):
    in_specs = (
        P(("row", "col"), None),
        P(),
        P(("row", "col"), None, None),
        P(("row", "col"), None),
        P(("row", "col")),
    )
    out_specs = P(("row", "col"), None)
    return jax.shard_map(local, mesh=mesh, in_specs=in_specs, out_specs=out_specs, check_vma=False)
```

profile of v0, /device:TPU:15, one launch (start us, length us, event | category | flops | bytes accessed | tf_op | source)
XLA Modules:
  0.0 800.6 jit_solution(2866157427274746892)
XLA Ops:
  6.5 0.7 all-gather.2.cloned.1.call-update
  7.3 61.3 %all-gather.2.cloned.1.call-done = bf16[2048,256]{1,0:T(8,128)(2,1)} async-done(((bf16[128,256]{1,0:T(8,128)(2,1)}), bf16[2048,256]{1,0:T(8,128)(2,1)}) %all-gather.2.cloned.1.call-update) | async-done | bytes 1048592 | tf_op jit(solution)/shard_map/all_gather | solution.py:27
  68.6 1.1 broadcast_select_fusion.1
  70.4 5.6 convert_bitcast_fusion
  76.0 11.4 %copy.11 = bf16[8,2048,256]{2,1,0:T(8,128)(2,1)} copy(bf16[8,2048,256]{1,2,0:T(8,128)(2,1)} %convert_bitcast_fusion) | data formatting | bytes 16777216 | tf_op jit(solution)/shard_map/while | solution.py:64
  87.4 128.8 %all-reduce.4.cloned.1.call-done = bf16[2048,256]{1,0:T(8,128)(2,1)} async-done(((bf16[2048,256]{1,0:T(8,128)(2,1)}), bf16[2048,256]{1,0:T(8,128)(2,1)}) %all-reduce.4.cloned.1.call-update) | async-done | bytes 1048592 | tf_op jit(solution)/shard_map/psum | solution.py:11
  216.2 6.8 convolution_convert_fusion
  223.0 1.5 broadcast.27.clone
  224.5 1.5 broadcast.27
  226.0 82.1 %while.12 = (s32[]{:T(128)}, f32[8,256,256]{2,1,0:T(8,128)}, f32[8,256,256]{2,1,0:T(8,128)}, s32[]{:T(128)}, s32[32,3]{0,1:T(4,128)S(1)}, /*index=5*/s32[]{:T(12...) while((s32[]{:T(128)}, f32[8,256,256]{2,1,0:T(8,128)}, ...), condition=%wide.region_4.5_spmd, body=%wide.region_1.4_spmd.sunk | while | flops 808453248 | bytes 39850920 | solution.py:64
  226.0 0.7 add_compare_fusion.2
  226.8 1.8 gather_fusion.1
  228.6 4.0 gather_fusion
  232.6 1.0 copy-done.1
  233.6 1.7 select_convert_fusion.2
  235.3 1.0 copy-done.2
  236.3 1.7 fusion.31
  238.1 4.2 scatter_fusion.1
  242.3 5.0 gather_fusion.2
  247.2 2.0 fusion.30
  249.2 4.2 scatter_fusion
  253.4 0.7 add_compare_fusion.2
  254.2 1.8 gather_fusion.1
  256.0 4.0 gather_fusion
  260.0 1.0 copy-done.1
  261.0 1.7 select_convert_fusion.2
  262.7 1.0 copy-done.2
  263.7 1.7 fusion.31
  265.4 4.2 scatter_fusion.1
  269.6 5.0 gather_fusion.2
  274.6 2.0 fusion.30
  276.6 4.2 scatter_fusion
  280.8 0.7 add_compare_fusion.2
  281.6 1.8 gather_fusion.1
  283.4 4.0 gather_fusion
  287.4 1.0 copy-done.1
  288.4 1.7 select_convert_fusion.2
  290.1 1.0 copy-done.2
  291.1 1.7 fusion.31
  292.9 4.1 scatter_fusion.1
  297.0 5.0 gather_fusion.2
  302.0 2.0 fusion.30
  303.9 4.2 scatter_fusion
  308.8 202.4 %all-reduce.6.cloned.1.call-done = f32[2048,256]{1,0:T(8,128)} async-done(((f32[2048,256]{1,0:T(8,128)}), f32[2048,256]{1,0:T(8,128)}) %all-reduce.6.cloned.1.call-update) | async-done | bytes 2097168 | tf_op jit(solution)/shard_map/psum | solution.py:67
  511.2 1.4 broadcast_select_fusion
  512.7 100.2 %reduce-scatter.2.cloned.1.call-done = f32[128,256]{1,0:T(8,128)} async-done(((f32[2048,256]{1,0:T(8,128)}), f32[128,256]{1,0:T(8,128)}) %reduce-scatter.2.cloned.1.call-update) | async-done | bytes 131088 | tf_op jit(solution)/shard_map/reduce_scatter | solution.py:68
  612.9 179.6 %all-reduce.8.cloned.1.call-done = f32[2048,256]{1,0:T(8,128)} async-done(((f32[2048,256]{1,0:T(8,128)}), f32[2048,256]{1,0:T(8,128)}) %all-reduce.8.cloned.1.call-update) | async-done | bytes 2097168 | tf_op jit(solution)/shard_map/psum | solution.py:11
  792.4 1.6 multiply_subtract_fusion
  (32 shorter events, 1.0 us)
Async XLA Ops:
  6.5 63.8 %copy-start = (bf16[8,256,256]{2,1,0:T(8,128)(2,1)S(1)}, bf16[8,256,256]{2,1,0:T(8,128)(2,1)}, u32[]{:S(2)}) copy-start(bf16[8,256,256]{2,1,0:T(8,128)(2,1)} %param.8) | copy-start | bytes 3145732
  6.5 62.0 %all-gather.2.cloned.1.call-start = ((), (), s32[]{:S(2)}) async-start(), calls=%async_computation.1 | async-start | bytes 1114112 | tf_op jit(solution)/shard_map/all_gather | solution.py:27
  7.3 208.9 %all-reduce.4.cloned.1.call-start = ((), (), s32[]{:S(2)}) async-start(), calls=%async_computation.2 | async-start | bytes 2097152 | tf_op jit(solution)/shard_map/psum | solution.py:11
  68.6 1.8 copy-start.3
  69.6 441.6 %all-reduce.6.cloned.1.call-start = ((), (), s32[]{:S(2)}) async-start(), calls=%async_computation.4 | async-start | bytes 4194304 | tf_op jit(solution)/shard_map/psum | solution.py:67
  223.0 3.0 copy-start.5
  232.6 1.0 copy-start.1
  235.3 1.0 copy-start.2
  260.0 1.0 copy-start.1
  262.7 1.0 copy-start.2
  287.4 1.0 copy-start.1
  290.1 1.0 copy-start.2
  308.1 304.7 %reduce-scatter.2.cloned.1.call-start = ((), (), s32[]{:S(2)}) async-start(), calls=%async_computation.3 | async-start | bytes 2228224 | tf_op jit(solution)/shard_map/reduce_scatter | solution.py:68
  308.7 483.7 %all-reduce.8.cloned.1.call-start = ((), (), s32[]{:S(2)}) async-start(), calls=%async_computation.5 | async-start | bytes 4194304 | tf_op jit(solution)/shard_map/psum | solution.py:11
  512.6 279.8 %copy-start.4 = (bf16[128,256]{1,0:T(8,128)(2,1)S(1)}, bf16[128,256]{1,0:T(8,128)(2,1)}, u32[]{:S(2)}) copy-start(bf16[128,256]{1,0:T(8,128)(2,1)} %param.7) | copy-start | bytes 196612
Sparse Core Ops, SparseCore 0:
  10.1 58.4 all-gather.1
  71.2 144.9 all-reduce.3
  308.3 202.8 all-reduce.5
  515.3 97.5 reduce-scatter.1
  615.4 177.0 all-reduce.7
where the time goes:
time: 809 us; the launch traced here: 801 us
  waiting for transfers between devices  673 us (83%)
  local copies, waits for them, and re-layouts  53 us (7%)
  other arithmetic  31.2 us (4%)
  matrix products  28.6 us (4%)
  between operations  13.8 us (2%)
    psum x2, waiting for transfers between devices, broadcast(): return lax.psum(kept, axis)  308 us
    psum x1, waiting for transfers between devices, local(): tgt_total = lax.psum(grad_tgt, 'row')  202 us
    reduce_scatter x1, waiting for transfers between devices, local(): summed = lax.psum_scatter(grad_src, 'col', scatter_dimension=0, tiled=True)  100 us
    all_gather x1, waiting for transfers between devices, local(): source = lax.all_gather(factors, 'col', axis=0, tiled=True)  61.3 us
  transfers between devices with their start and end apart: 5, of which 5 were waited for; matrix products, arithmetic and copies ran while one was open for 2% of the time, Pallas kernels for 0%

commit v1 on v0

v1 whole, which is shorter than its diff:
```python
import jax
import jax.numpy as jnp
from jax import lax
from jax.experimental import pallas as pl
from jax.experimental.pallas import tpu as pltpu
from jax.sharding import PartitionSpec as P

weight_decay = 1.0
MESH = pl.DeviceIdType.MESH
ROWS = 128
HALF = 64
TILE = 256
CAP = 32
F32 = jnp.float32
BF16 = jnp.bfloat16


class Place:
    def __init__(self):
        row, col = lax.axis_index("row"), lax.axis_index("col")
        self.row, self.col = row, col
        self.x, self.zl = row // 4, row % 4
        self.zh, self.y, self.c = col // 8, (col // 2) % 4, col % 2

    def at_row(self, x, zl):
        return ((x % 4) * 4 + zl % 4, self.col)

    def at_col(self, zh, y, c):
        return (self.row, zh * 8 + (y % 4) * 2 + c)

    def meet(self):
        x, zl, zh, y, c = self.x, self.zl, self.zh, self.y, self.c
        self.xp, self.xm = self.at_row(x + 1, zl), self.at_row(x + 3, zl)
        self.zls = [self.at_row(x, zl + d) for d in (1, 2, 3)]
        self.yp, self.ym = self.at_col(zh, y + 1, c), self.at_col(zh, y + 3, c)
        self.far = self.at_col(1 - zh, y, c)
        self.core = self.at_col(zh, y, 1 - c)
        self.flip = (self.col, self.row)
        barrier = pltpu.get_barrier_semaphore()
        peers = [self.xp, self.xm, *self.zls, self.yp, self.ym, self.far, self.core]
        for peer in peers:
            pl.semaphore_signal(barrier, inc=1, device_id=peer, device_id_type=MESH)

        @pl.when(self.row != self.col)
        def _():
            pl.semaphore_signal(barrier, inc=1, device_id=self.flip, device_id_type=MESH)

        pl.semaphore_wait(barrier, len(peers) + jnp.where(self.row != self.col, 1, 0))


class Wires:
    def __init__(self, ssem, rsem):
        self.ssem, self.rsem, self.sent = ssem, rsem, []

    def make(self, n, src, dst, device):
        return pltpu.make_async_remote_copy(
            src_ref=src,
            dst_ref=dst,
            send_sem=self.ssem.at[n],
            recv_sem=self.rsem.at[n],
            device_id=device,
            device_id_type=MESH,
        )

    def send(self, n, src, dst, device):
        copy = self.make(n, src, dst, device)
        copy.start()
        self.sent.append(copy)

    def landed(self, n, dst, device):
        self.make(n, dst, dst, device).wait_recv()

    def drain(self):
        for copy in self.sent:
            copy.wait_send()


def slot(ref, index, first=0, size=ROWS):
    return ref.at[pl.ds(pl.multiple_of(index * ROWS + first, HALF), size), :]


def gather_kernel(fac, src, tgt, ssem, rsem):
    p = Place()
    p.meet()
    w = Wires(ssem, rsem)
    x, zl, zh, y, c, row, col = p.x, p.zl, p.zh, p.y, p.c, p.row, p.col
    T, FAR, CORE, ZL, YD, YR, XD, XR = 0, 1, 2, 10, 13, 17, 21, 29
    off_diag = row != col
    turn = w.make(T, fac, slot(tgt, row * 0 + col), p.flip)

    @pl.when(off_diag)
    def _():
        turn.start()

    w.send(FAR, fac, slot(src, col), p.far)
    w.send(YD + 0, fac, slot(src, col), p.yp)
    w.send(YD + 1, fac, slot(src, col), p.ym)
    w.send(CORE + 0, fac, slot(src, col), p.core)
    src[pl.ds(pl.multiple_of(col * ROWS, ROWS), ROWS), :] = fac[...]

    @pl.when(row == col)
    def _():
        tgt[pl.ds(pl.multiple_of(row * ROWS, ROWS), ROWS), :] = fac[...]

    @pl.when(off_diag)
    def _():
        w.landed(T, slot(tgt, row), p.flip)

    mine = slot(tgt, row)
    w.send(XD + 0, mine, mine, p.xp)
    w.send(XD + 1, mine, mine, p.xm)
    for d in (1, 2, 3):
        w.send(ZL + d - 1, mine, mine, p.zls[d - 1])

    def at(yy, hh):
        return hh * 8 + (yy % 4) * 2 + c

    def y_pass(h, hh, core_base):
        left, right, far = at(y + 3, hh), at(y + 1, hh), at(y + 2, hh)
        w.landed(YD + 2 * h, slot(src, left), p.ym)
        w.send(YR + 2 * h, slot(src, left, 0, HALF), slot(src, left, 0, HALF), p.yp)
        w.send(core_base, slot(src, left), slot(src, left), p.core)
        w.landed(YD + 2 * h + 1, slot(src, right), p.yp)
        w.send(YR + 2 * h + 1, slot(src, right, HALF, HALF), slot(src, right, HALF, HALF), p.ym)
        w.send(core_base + 1, slot(src, right), slot(src, right), p.core)

    def y_last(h, hh, core_base):
        far = at(y + 2, hh)
        w.landed(YR + 2 * h, slot(src, far, 0, HALF), p.ym)
        w.landed(YR + 2 * h + 1, slot(src, far, HALF, HALF), p.yp)
        w.send(core_base + 2, slot(src, far), slot(src, far), p.core)

    w.landed(FAR, slot(src, at(y, 1 - zh)), p.far)
    other = slot(src, at(y, 1 - zh))
    w.send(YD + 2, other, other, p.yp)
    w.send(YD + 3, other, other, p.ym)
    w.send(CORE + 1, other, other, p.core)
    y_pass(0, zh, CORE + 2)
    for d in (1, 2, 3):
        got = slot(tgt, x * 4 + (zl + 4 - d) % 4)
        w.landed(ZL + d - 1, got, p.zls[3 - d])
        w.send(XD + 2 * d, got, got, p.xp)
        w.send(XD + 2 * d + 1, got, got, p.xm)
    for d in (0, 1, 2, 3):
        k = (zl + 4 - d) % 4
        left, right = ((x + 3) % 4) * 4 + k, ((x + 1) % 4) * 4 + k
        w.landed(XD + 2 * d, slot(tgt, left), p.xm)
        w.send(XR + 2 * d, slot(tgt, left, 0, HALF), slot(tgt, left, 0, HALF), p.xp)
        w.landed(XD + 2 * d + 1, slot(tgt, right), p.xp)
        w.send(XR + 2 * d + 1, slot(tgt, right, HALF, HALF), slot(tgt, right, HALF, HALF), p.xm)
        if d == 0:
            y_pass(1, 1 - zh, CORE + 5)
            y_last(0, zh, CORE + 2)
            y_last(1, 1 - zh, CORE + 5)
    for d in (0, 1, 2, 3):
        far = ((x + 2) % 4) * 4 + (zl + 4 - d) % 4
        w.landed(XR + 2 * d, slot(tgt, far, 0, HALF), p.xm)
        w.landed(XR + 2 * d + 1, slot(tgt, far, HALF, HALF), p.xp)

    def partner(yy, hh):
        return slot(src, hh * 8 + (yy % 4) * 2 + 1 - c)

    arrivals = [(y, zh), (y, 1 - zh)]
    arrivals += [(y + d, hh) for hh in (zh, 1 - zh) for d in (3, 1, 2)]
    for n, (yy, hh) in enumerate(arrivals):
        w.landed(CORE + n, partner(yy, hh), p.core)

    @pl.when(off_diag)
    def _():
        turn.wait_send()

    w.drain()


def tile_kernel(coords, count, src, tgt, cores, tiles, gsrc, gtgt, held, sem):
    live = count[0]
    for s in range(CAP):
        @pl.when(s < live)
        def _():
            pltpu.make_async_copy(tiles.at[s], held.at[s], sem.at[s]).start()

    gsrc[...] = jnp.zeros_like(gsrc)
    gtgt[...] = jnp.zeros_like(gtgt)

    def rows(i):
        return pl.ds(pl.multiple_of(i * TILE, TILE), TILE)

    def dot(a, b, ca, cb):
        return lax.dot_general(a, b, (((ca,), (cb,)), ((), ())), preferred_element_type=F32)

    def step(i, _):
        s = [2 * i, 2 * i + 1]
        for u in s:
            @pl.when(u < live)
            def _():
                pltpu.make_async_copy(tiles.at[u], held.at[u], sem.at[u]).wait()
        rel = [cores[coords[u * 3 + 0]] for u in s]
        a = [rows(coords[u * 3 + 1]) for u in s]
        b = [rows(coords[u * 3 + 2]) for u in s]
        left = [dot(src[a[n], :], rel[n], 1, 0).astype(BF16) for n in (0, 1)]
        right = [dot(tgt[b[n], :], rel[n], 1, 1).astype(BF16) for n in (0, 1)]
        resid = []
        for n in (0, 1):
            predicted = dot(left[n], tgt[b[n], :], 1, 1)
            diff = held[s[n]].astype(F32) - predicted
            resid.append(jnp.where(s[n] < live, diff, 0.0).astype(BF16))
        for n in (0, 1):
            gsrc[a[n], :] += dot(resid[n], right[n], 1, 0)
            gtgt[b[n], :] += dot(resid[n], left[n], 0, 0)
        return 0

    lax.fori_loop(0, (live + 1) // 2, step, 0)


def reduce_kernel(fac, src, tgt, out, xrelay, xdone, zin, core_in, yrelay, ydone, send_z, far_in, send_f, send_t, turn_in, ssem, rsem):
    p = Place()
    p.meet()
    w = Wires(ssem, rsem)
    x, zl, zh, y, c, row, col = p.x, p.zl, p.zh, p.y, p.c, p.row, p.col
    off_diag = row != col
    XS, XA, XD, ZL, CORE, YS, YA, YD, FAR, T = 0, 8, 16, 24, 27, 35, 39, 43, 47, 48
    A, B = 0, HALF

    def part(ref, index, first=0, size=ROWS):
        return ref[pl.ds(pl.multiple_of(index * ROWS + first, HALF), size), :]

    def xs(q, d):
        return ((x + q) % 4) * 4 + (zl + d) % 4

    order = (1, 2, 3, 0)
    for d in order:
        w.send(XS + 2 * d, slot(tgt, xs(2, d), A, HALF), xrelay.at[2 * d], p.xp)
        w.send(XS + 2 * d + 1, slot(tgt, xs(2, d), B, HALF), xrelay.at[2 * d + 1], p.xm)
    for d in order:
        w.send(XD + 2 * d, slot(tgt, xs(1, d), B, HALF), xdone.at[4 * d + 0], p.xp)
        w.send(XD + 2 * d + 1, slot(tgt, xs(3, d), A, HALF), xdone.at[4 * d + 1], p.xm)

    def ys(q, h, cc):
        return ((zh + h) % 2) * 8 + ((y + q) % 4) * 2 + cc

    quarters = (2, 1, 3, 0)
    for n, q in enumerate(quarters):
        for h in (1, 0):
            m = 2 * n + h
            w.send(CORE + m, slot(src, ys(q, h, 1 - c)), core_in.at[m], p.core)
    for n, q in enumerate(quarters):
        for h in (1, 0):
            m = 2 * n + h
            w.landed(CORE + m, core_in.at[m], p.core)
            core_in[m] += part(src, ys(q, h, c))
            if q == 2:
                w.send(YS + 2 * h, core_in.at[m, pl.ds(A, HALF), :], yrelay.at[2 * h], p.yp)
                w.send(YS + 2 * h + 1, core_in.at[m, pl.ds(B, HALF), :], yrelay.at[2 * h + 1], p.ym)
            if q == 1:
                w.send(YD + 2 * h, core_in.at[m, pl.ds(B, HALF), :], ydone.at[4 * h + 0], p.yp)
            if q == 3:
                w.send(YD + 2 * h + 1, core_in.at[m, pl.ds(A, HALF), :], ydone.at[4 * h + 1], p.ym)
    for d in order:
        w.landed(XS + 2 * d, xrelay.at[2 * d], p.xm)
        xrelay[2 * d] += part(tgt, xs(1, d), A, HALF)
        w.send(XA + 2 * d, xrelay.at[2 * d], xdone.at[4 * d + 2], p.xp)
        w.landed(XS + 2 * d + 1, xrelay.at[2 * d + 1], p.xp)
        xrelay[2 * d + 1] += part(tgt, xs(3, d), B, HALF)
        w.send(XA + 2 * d + 1, xrelay.at[2 * d + 1], xdone.at[4 * d + 3], p.xm)
    for h in (1, 0):
        w.landed(YS + 2 * h, yrelay.at[2 * h], p.ym)
        yrelay[2 * h] += core_in[2 + h, pl.ds(A, HALF), :]
        w.send(YA + 2 * h, yrelay.at[2 * h], ydone.at[4 * h + 2], p.yp)
        w.landed(YS + 2 * h + 1, yrelay.at[2 * h + 1], p.yp)
        yrelay[2 * h + 1] += core_in[4 + h, pl.ds(B, HALF), :]
        w.send(YA + 2 * h + 1, yrelay.at[2 * h + 1], ydone.at[4 * h + 3], p.ym)

    def y_sum(h):
        w.landed(YD + 2 * h, ydone.at[4 * h + 0], p.ym)
        w.landed(YD + 2 * h + 1, ydone.at[4 * h + 1], p.yp)
        w.landed(YA + 2 * h, ydone.at[4 * h + 2], p.ym)
        w.landed(YA + 2 * h + 1, ydone.at[4 * h + 3], p.yp)
        own = core_in[6 + h]
        top = own[:HALF] + ydone[4 * h + 1] + ydone[4 * h + 2]
        low = own[HALF:] + ydone[4 * h + 0] + ydone[4 * h + 3]
        return jnp.concatenate([top, low], axis=0)

    def x_sum(d):
        w.landed(XD + 2 * d, xdone.at[4 * d + 0], p.xm)
        w.landed(XD + 2 * d + 1, xdone.at[4 * d + 1], p.xp)
        w.landed(XA + 2 * d, xdone.at[4 * d + 2], p.xm)
        w.landed(XA + 2 * d + 1, xdone.at[4 * d + 3], p.xp)
        own = part(tgt, xs(0, d))
        top = own[:HALF] + xdone[4 * d + 1] + xdone[4 * d + 2]
        low = own[HALF:] + xdone[4 * d + 0] + xdone[4 * d + 3]
        return jnp.concatenate([top, low], axis=0)

    send_f[...] = y_sum(1)
    w.send(FAR, send_f, far_in, p.far)
    for d in (1, 2, 3):
        send_z[d - 1] = x_sum(d)
        w.send(ZL + d - 1, send_z.at[d - 1], zin.at[d - 1], p.zls[d - 1])
    total = x_sum(0)
    for d in (1, 2, 3):
        w.landed(ZL + d - 1, zin.at[d - 1], p.zls[3 - d])
        total = total + zin[d - 1]
    send_t[...] = total
    turn = w.make(T, send_t, turn_in, p.flip)

    @pl.when(off_diag)
    def _():
        turn.start()

    @pl.when(row == col)
    def _():
        turn_in[...] = send_t[...]

    near = y_sum(0)
    w.landed(FAR, far_in, p.far)
    near = near + far_in[...]

    @pl.when(off_diag)
    def _():
        turn.wait()

    summed = near + turn_in[...]
    out[...] = weight_decay * fac[...].astype(F32) - summed * (1.0 / TILE)
    w.drain()


def local(factors, cores, tiles, tile_coords, tile_counts):
    vmem = pl.BlockSpec(memory_space=pltpu.VMEM)
    smem = pl.BlockSpec(memory_space=pltpu.SMEM)
    hbm = pl.BlockSpec(memory_space=pl.ANY)
    dma = pltpu.SemaphoreType.DMA
    rank = factors.shape[1]
    block = 16 * ROWS
    src, tgt = pl.pallas_call(
        gather_kernel,
        out_shape=(jax.ShapeDtypeStruct((block, rank), BF16),) * 2,
        in_specs=[vmem],
        out_specs=(vmem, vmem),
        scratch_shapes=[dma((37,)), dma((37,))],
        compiler_params=pltpu.CompilerParams(collective_id=0, has_side_effects=True),
        name="gather",
    )(factors)
    gsrc, gtgt = pl.pallas_call(
        tile_kernel,
        out_shape=(jax.ShapeDtypeStruct((block, rank), F32),) * 2,
        in_specs=[smem, smem, vmem, vmem, vmem, hbm],
        out_specs=(vmem, vmem),
        scratch_shapes=[pltpu.VMEM((CAP, TILE, TILE), BF16), dma((CAP,))],
        name="tiles",
    )(tile_coords.reshape(-1), tile_counts, src, tgt, cores, tiles)
    full, half = (ROWS, rank), (HALF, rank)
    return pl.pallas_call(
        reduce_kernel,
        out_shape=jax.ShapeDtypeStruct(full, F32),
        in_specs=[vmem, vmem, vmem],
        out_specs=vmem,
        scratch_shapes=[
            pltpu.VMEM((8, *half), F32),
            pltpu.VMEM((16, *half), F32),
            pltpu.VMEM((3, *full), F32),
            pltpu.VMEM((8, *full), F32),
            pltpu.VMEM((4, *half), F32),
            pltpu.VMEM((8, *half), F32),
            pltpu.VMEM((3, *full), F32),
            pltpu.VMEM(full, F32),
            pltpu.VMEM(full, F32),
            pltpu.VMEM(full, F32),
            pltpu.VMEM(full, F32),
            dma((49,)),
            dma((49,)),
        ],
        compiler_params=pltpu.CompilerParams(collective_id=1, has_side_effects=True),
        name="reduce",
    )(factors, gsrc, gtgt)


def solution(mesh):
    in_specs = (
        P(("row", "col"), None),
        P(),
        P(("row", "col"), None, None),
        P(("row", "col"), None),
        P(("row", "col")),
    )
    out_specs = P(("row", "col"), None)
    return jax.shard_map(local, mesh=mesh, in_specs=in_specs, out_specs=out_specs, check_vma=False)
```

time: 809 us -> 102 us (0.13); the launches traced: 801 us -> 102 us
  waiting for transfers between devices: 673 us -> 0 us
  Pallas kernels: 0 us -> 98.5 us
  local copies, waits for them, and re-layouts: 53 us -> 2.95 us
  other arithmetic: 31.2 us -> 0 us
  matrix products: 28.6 us -> 0 us
  between operations: 13.8 us -> 0.68 us
    psum x3 -> x0, waiting for transfers between devices: 511 us -> none  [the longest x2 308 us: broadcast(): return lax.psum(kept, axis)]
    reduce_scatter x1 -> x0, waiting for transfers between devices: 100 us -> none  [local(): summed = lax.psum_scatter(grad_src, 'col', scatter_dimension=0, tiled=True)]
    pallas_call x0 -> x3, Pallas kernels: none -> 98.5 us  [the longest x1 54.2 us: local(): pl.pallas_call(reduce_kernel, out_shape=jax.ShapeDtypeStruct(full, F32),...]
    all_gather x1 -> x0, waiting for transfers between devices: 61.3 us -> none  [local(): source = lax.all_gather(factors, 'col', axis=0, tiled=True)]
    gather x9 -> x0, local copies, waits for them, and re-layouts: 32.5 us -> none  [the longest x3 14.9 us: group_pass(): right_rel = right_core[relation, tgt_index]]
    dot_general x11 -> x0, matrix products: 28.6 us -> none  [the longest x1 6.82 us: local(): jnp.einsum('nr,ksr->kns', received, cores, preferred_element_type=jnp.flo...]
    scatter-add x6 -> x0, other arithmetic: 25.1 us -> none  [the longest x3 12.6 us: group_pass(): grad_src.at[src_index].add(src_grad)]
    while x13 -> x0, local copies, waits for them, and re-layouts: 17.3 us -> none  [the longest x1 11.4 us: local(): lax.fori_loop(0, (live_count + 7) // 8, group_pass, start_grads)]
  transfers between devices with their start and end apart: 5 -> 0, of which waited for: 5 -> 0; matrix products, arithmetic and copies ran while one was open for 2% -> 0% of each run, Pallas kernels for 0% -> 0%
where the time goes in v1:
time: 102 us
  Pallas kernels  98.5 us (97%)
  local copies, waits for them, and re-layouts  2.95 us (3%)
    pallas_call x1, Pallas kernels, local(): pl.pallas_call(reduce_kernel, out_shape=jax.ShapeDtypeStruct(full, F32),...  54.2 us
    pallas_call x1, Pallas kernels, local(): pl.pallas_call(gather_kernel, out_shape=(jax.ShapeDtypeStruct((block, ran...  30.4 us
    pallas_call x1, Pallas kernels, local(): pl.pallas_call(tile_kernel, out_shape=(jax.ShapeDtypeStruct((block, rank)...  13.8 us
    unnamed x2, local copies, waits for them, and re-layouts  2.33 us

profile of v1, /device:TPU:15, one launch (start us, length us, event | category | flops | bytes accessed | tf_op | source)
XLA Modules:
  0.0 102.1 jit_solution(204201697489800636)
XLA Ops:
  0.7 0.8 copy.7
  1.4 0.6 reshape.3.coords
  2.0 30.4 %gather.1 = (bf16[2048,256]{1,0:T(8,128)(2,1)}, bf16[2048,256]{1,0:T(8,128)(2,1)}) custom-call(bf16[128,256]{1,0:T(8,128)(2,1)} %fac.3), custom_call_target="tpu_custom_call" | custom-call | tf_op jit(solution)/shard_map/gather/pallas_call | solution.py:333
  32.5 13.8 %tiles.2 = (f32[2048,256]{1,0:T(8,128)}, f32[2048,256]{1,0:T(8,128)}) custom-call(s32[96]{0:T(128)} %reshape.3.coords, s32[1]{0:T(128)S(6)} %copy.9.count, bf16[2048,256]{1,0:T(8,128)(2,1)} %get-tuple-element.9.src, bf16[2048,256]{1,0:T(8,128)(2,1)} %get-tuple-element.10.tgt, bf16[8,256,256]{2,1,0:T(8,128)(2,1)} %cores.1, bf16[32,256,256]{2,1,0:T(8,128)(2,1)} %tiles.3), custom_call_target="tpu_custom_call" | custom-call | tf_op jit(solution)/shard_map/tiles/pallas_call | solution.py:342
  46.3 54.2 %reduce.1 = f32[128,256]{1,0:T(8,128)} custom-call(bf16[128,256]{1,0:T(8,128)(2,1)} %fac.3, f32[2048,256]{1,0:T(8,128)} %get-tuple-element.11.src, f32[2048,256]{1,0:T(8,128)} %get-tuple-element.12.tgt), custom_call_target="tpu_custom_call" | custom-call | tf_op jit(solution)/shard_map/reduce/pallas_call | solution.py:351
  100.5 1.6 %copy.10 = f32[128,256]{1,0:T(8,128)} copy(f32[128,256]{1,0:T(8,128)} %reduce.1) | data formatting | bytes 262144
